TPU v7x, 256 devices: a whole 4x4x8 slice. The times are simulated.
256 devices in a mesh: crop: 2 (over core), row: 8 (over x_hi, y), col: 16 (over z, x_lo).
Axes of the slice: x: 4 (x_hi: 2, x_lo: 2; x = x_hi * 2 + x_lo), y: 4, z: 8, core: 2. Of those that a mesh axis runs over, the one named last changes fastest.
Arguments:
- pair_state: bfloat16 [768, 384, 128], P(('crop', 'row'), 'col'), parts along dimension 0, may hold values from -6 to 6
- token_mask: int32 [768], P('crop'), parts along dimension 0, may hold values from 0 to 1, as said below
- block_pattern: int32 [8, 4], P('crop'), parts along dimension 0, may hold values from 0 to 1, as said below
- triangle_norm: float32 [128], replicated, may hold values from 0.1 to 1.9
- triangle_input: bfloat16 [128, 512], replicated, may hold values from -0.5 to 0.5
- triangle_gate: bfloat16 [128, 128], replicated, may hold values from -0.5 to 0.5
- product_norm: float32 [128], replicated, may hold values from 0.1 to 1.9
- triangle_output: bfloat16 [128, 128], replicated, may hold values from -0.5 to 0.5
- attend_norm: float32 [128], replicated, may hold values from 0.1 to 1.9
- attend_inputs: bfloat16 [128, 384], replicated, may hold values from -4 to 4
- attend_gate: bfloat16 [128, 128], replicated, may hold values from -0.5 to 0.5
- attend_bias: bfloat16 [128, 4], replicated, may hold values from -0.5 to 0.5
- attend_output: bfloat16 [128, 128], replicated, may hold values from -0.5 to 0.5
Outputs:
- pair_output: bfloat16 [768, 384, 128], P(('crop', 'row'), 'col'), parts along dimension 0
There are 2 independent parts, one for each index of `crop`. A program takes and returns all parts, laid end to end along the dimension named above; an argument that names none is the same for every part. Nothing has to cross between parts.
Inputs may be any that keep to these rules, and one draw needn't show every extreme that they name: `token_mask`: 1 on a prefix of 96 or more tokens and 0 after it. `block_pattern`: every row allows its own block and block 0.
All inputs are finite; a program needn't handle non-finite values.
Results may differ from a plain program's by a relative error of at most 0.02.
Values may be sent and summed in bfloat16 or wider, within the bound.
A program may use at most 64 MiB of HBM per device.

v0:
```python
import math
import jax
import jax.numpy as jnp
from jax import lax
from jax.sharding import Mesh
from jax.sharding import PartitionSpec as P

ROW = ("row_0", "row_1")
COL = ("col_0", "col_1")
ROW_COL = ("row_0", "row_1", "col_0", "col_1")
CROP_ROW = ("crop", "row_0", "row_1")
norm_epsilon = 1e-05


def joined_along(pieces, dim):
    lengths = list(pieces.shape[1:])
    lengths[dim] *= pieces.shape[0]
    return jnp.moveaxis(pieces, 0, dim).reshape(lengths)


def gather_in_order(array, axes, turns):
    pieces = array[None]
    for k in turns:
        pieces = lax.all_gather(pieces, axes[k], axis=0, tiled=True)
    held = [lax.axis_size(axes[k]) for k in reversed(turns)]
    pieces = pieces.reshape(*held, *array.shape)
    turned = sorted(range(len(turns)), key=lambda place: turns[len(turns) - 1 - place])
    return pieces.transpose(*turned, *range(len(turns), pieces.ndim)).reshape(-1, *array.shape)


def whole_of(array, axes, turns, dim):
    return joined_along(gather_in_order(array, axes, turns), dim)


def layer_norm(inputs, gain):
    average = jnp.mean(inputs, axis=-1, keepdims=True)
    centered = inputs - average
    variance = jnp.mean(centered * centered, axis=-1, keepdims=True)
    return centered * lax.rsqrt(variance + norm_epsilon) * gain


def project_rows(pair_rows, attend_inputs, attend_gate, head_count):
    row_count, token_count, channels = pair_rows.shape
    head_width = channels // head_count
    combined = jnp.dot(pair_rows, attend_inputs, preferred_element_type=jnp.float32)
    queries = (
        combined[..., :channels]
        .astype(jnp.bfloat16)
        .reshape(row_count, token_count, head_count, head_width)
    )
    key_rows = (
        combined[..., channels : 2 * channels]
        .astype(jnp.bfloat16)
        .reshape(row_count, token_count, head_count, head_width)
    )
    values = (
        combined[..., 2 * channels :]
        .astype(jnp.bfloat16)
        .reshape(row_count, token_count, head_count, head_width)
    )
    gate_values = jax.nn.sigmoid(
        jnp.dot(pair_rows, attend_gate, preferred_element_type=jnp.float32)
    )
    return (queries, key_rows, values, gate_values)


def attend_dense(pair_rows, attend_inputs, attend_gate, head_bias, allowed):
    row_count, token_count, channels = pair_rows.shape
    head_count = head_bias.shape[0]
    queries, key_rows, values, gate_values = project_rows(
        pair_rows, attend_inputs, attend_gate, head_count
    )
    scores = jnp.einsum(
        "rjhd,rkhd->rhjk", queries, key_rows, preferred_element_type=jnp.float32
    ) / math.sqrt(channels // head_count)
    scores = scores + head_bias.astype(jnp.float32)[None]
    scores = jnp.where(allowed[None, None], scores, -jnp.inf)
    row_max = jnp.max(scores, axis=-1, keepdims=True)
    weights = jnp.exp(scores - row_max)
    probabilities = (weights / jnp.sum(weights, axis=-1, keepdims=True)).astype(jnp.bfloat16)
    attended = jnp.einsum(
        "rhjk,rkhd->rjhd", probabilities, values, preferred_element_type=jnp.float32
    ).reshape(row_count, token_count, channels)
    return (gate_values * attended).astype(jnp.bfloat16)


def shards(
    pair_state,
    token_mask,
    block_pattern,
    triangle_norm,
    triangle_input,
    triangle_gate,
    product_norm,
    triangle_output,
    attend_norm,
    attend_inputs,
    attend_gate,
    attend_bias,
    attend_output,
):
    tile_rows, tile_columns, channels = pair_state.shape
    row_devices = lax.axis_size(ROW)
    column_devices = lax.axis_size(COL)
    token_count = tile_columns * column_devices
    row_index = lax.axis_index(ROW)
    column_index = lax.axis_index(COL)
    valid_tokens = token_mask.astype(jnp.float32)
    row_valid = lax.dynamic_slice_in_dim(valid_tokens, row_index * tile_rows, tile_rows)
    column_valid = lax.dynamic_slice_in_dim(valid_tokens, column_index * tile_columns, tile_columns)
    state_float = pair_state.astype(jnp.float32)
    normed = layer_norm(state_float, triangle_norm).astype(jnp.bfloat16)
    projected = jnp.dot(normed, triangle_input, preferred_element_type=jnp.float32)
    pair_valid = (row_valid[:, None] * column_valid[None, :])[:, :, None]
    left_factor = (
        pair_valid
        * jax.nn.sigmoid(projected[..., :channels])
        * projected[..., channels : 2 * channels]
    ).astype(jnp.bfloat16)
    right_factor = (
        pair_valid
        * jax.nn.sigmoid(projected[..., 2 * channels : 3 * channels])
        * projected[..., 3 * channels :]
    ).astype(jnp.bfloat16)
    right_columns = lax.all_gather(right_factor, ROW, axis=0, tiled=True)
    summed_part = lax.dot_general(
        right_columns, left_factor, (((1,), (1,)), ((2,), (2,))), preferred_element_type=jnp.float32
    )
    flipped = lax.psum_scatter(
        jnp.transpose(summed_part, (1, 2, 0)), COL, scatter_dimension=0, tiled=True
    )
    product = jnp.transpose(flipped, (1, 0, 2))
    product_normed = layer_norm(product, product_norm).astype(jnp.bfloat16)
    gate_values = jax.nn.sigmoid(jnp.dot(normed, triangle_gate, preferred_element_type=jnp.float32))
    middle = (
        state_float
        + gate_values * jnp.dot(product_normed, triangle_output, preferred_element_type=jnp.float32)
    ).astype(jnp.bfloat16)
    attend_normed = layer_norm(middle.astype(jnp.float32), attend_norm).astype(jnp.bfloat16)
    head_count = attend_bias.shape[1]
    bias_tile = jnp.dot(attend_normed, attend_bias, preferred_element_type=jnp.float32).astype(
        jnp.bfloat16
    )
    flat_bias = jnp.transpose(bias_tile, (2, 0, 1)).reshape(head_count, tile_rows * tile_columns)
    gathered = whole_of(flat_bias, ROW_COL, (0, 3, 1, 2), 1)
    head_bias = gathered.reshape(head_count, row_devices, column_devices, tile_rows, tile_columns)
    head_bias = jnp.transpose(head_bias, (0, 1, 3, 2, 4)).reshape(
        head_count, token_count, token_count
    )
    blocks = block_pattern.shape[0]
    block_width = token_count // blocks
    pattern_ok = block_pattern[:, None, :, None] > 0
    allowed = jnp.broadcast_to(pattern_ok, (blocks, block_width, blocks, block_width)).reshape(
        token_count, token_count
    ) & (token_mask[None, :] > 0)
    rows_each = tile_rows // column_devices
    grouped = attend_normed.reshape(column_devices, rows_each, tile_columns, channels)
    received = lax.all_to_all(grouped, COL, split_axis=0, concat_axis=2, tiled=True)
    outer, inner, tokens_here, width_here = received.shape
    flat = received.reshape(outer * inner, tokens_here, width_here)
    attended_rows = attend_dense(flat, attend_inputs, attend_gate, head_bias, allowed).reshape(
        outer, inner, tokens_here, width_here
    )
    returned = lax.all_to_all(attended_rows, COL, split_axis=2, concat_axis=0, tiled=True)
    returned = returned.reshape(tile_rows, tile_columns, channels)
    update = jnp.dot(returned, attend_output, preferred_element_type=jnp.float32)
    return (middle.astype(jnp.float32) + update).astype(jnp.bfloat16)


def solution(mesh):
    finer = Mesh(
        mesh.devices.reshape(mesh.shape["crop"], 2, 4, 8, 2),
        ("crop", "row_0", "row_1", "col_0", "col_1"),
    )
    return jax.shard_map(
        shards,
        mesh=finer,
        in_specs=(
            P(CROP_ROW, COL, None),
            P("crop"),
            P("crop", None),
            P(),
            P(),
            P(),
            P(),
            P(),
            P(),
            P(),
            P(),
            P(),
            P(),
        ),
        out_specs=P(CROP_ROW, COL, None),
        check_vma=False,
    )
```

profile of v0, /device:TPU:8, one launch (start us, length us, event | category | flops | bytes accessed | tf_op | source)
XLA Modules:
  0.0 430.4 jit_solution(2989985232182543160)
XLA Ops:
  6.5 0.7 convert_element_type.68
  7.3 0.1 dynamic_slice.6
  7.3 0.1 dynamic_slice.7
  7.4 1.2 convert_reduce_fusion
  8.6 1.4 fusion.25
  10.0 0.1 broadcast_multiply_fusion
  10.1 1.5 fusion.39
  11.6 1.1 fusion.28
  12.7 0.0 all-gather.3.cloned.1.call-update
  12.7 0.0 reduce-scatter.2.cloned.1.call-start
  12.8 0.5 copy.85
  13.2 61.9 %all-gather.3.cloned.1.call-done = bf16[384,24,128]{2,1,0:T(8,128)(2,1)} async-done(((bf16[48,24,128]{2,1,0:T(8,128)(2,1)}), bf16[384,24,128]{2,1,0:T(8,128)(2,1)}) %all-gather.3.cloned.1.call-update) | async-done | bytes 2359312 | tf_op jit(solution)/shard_map/all_gather | solution.py:125
  75.1 3.7 copy.84
  78.8 5.1 %convolution_bitcast_fusion = f32[384,48,128]{0,1,2:T(8,128)} fusion(bf16[384,24,128]{0,1,2:T(8,128)(2,1)S(1)} %copy.84, bf16[48,24,128]{0,1,2:T(8,128)(2,1)S(1)} %copy.85), kind=kOutput, calls=%fused_computation.10 | convolution fusion | flops 113246208 | bytes 12091392 | tf_op jit(solution)/shard_map/dot_general | solution.py:126
  83.9 9.8 %copy.86 = f32[384,48,128]{2,1,0:T(8,128)} copy(f32[384,48,128]{0,1,2:T(8,128)} %convolution_bitcast_fusion) | data formatting | bytes 18874368 | tf_op jit(solution)/shard_map/transpose | solution.py:130
  93.7 0.0 copy-start.4
  93.8 0.0 copy-start.11
  93.8 0.0 copy-start.8
  93.8 0.0 reduce-scatter.2.cloned.1.call-update
  93.8 0.0 copy-start.7
  93.8 0.0 copy-start.6
  93.8 0.0 copy-start.3
  93.8 0.0 all-gather.5.cloned.1.call-start
  93.9 0.8 copy-done.2
  94.7 0.5 fusion.14
  95.2 201.7 %reduce-scatter.2.cloned.1.call-done = f32[24,48,128]{2,1,0:T(8,128)} async-done(((f32[384,48,128]{2,1,0:T(8,128)}), f32[24,48,128]{2,1,0:T(8,128)}) %reduce-scatter.2.cloned.1.call-update) | async-done | bytes 589840 | tf_op jit(solution)/shard_map/reduce_scatter | solution.py:129
  296.9 1.3 bitcast_reduce_fusion
  298.2 0.1 copy.87
  298.3 0.1 copy.88
  298.4 1.5 multiply_reduce_fusion.1
  299.9 0.1 copy.89
  300.0 0.1 copy.90
  300.0 1.4 multiply_convert_fusion.1
  301.5 0.4 fusion.52
  301.9 0.4 multiply_reduce_fusion
  302.3 1.1 multiply_convert_fusion
  303.4 1.6 fusion.20
  305.0 0.1 broadcast_in_dim_reshape.3
  305.1 5.9 %all_gather.16 = bf16[2,4,1152]{2,1,0:T(4,128)(2,1)S(1)} all-gather(bf16[1,4,1152]{2,1,0:T(4,128)(2,1)S(1)} %broadcast_in_dim_reshape.3), channel_id=1, replica_groups=mesh['crop'=2,'row_0'=2,'row_1'=4,'col_0'=8,'col_1'=2] {'row_0'}, dimensions={0}, use_global_device_ids=true | all-gather | bytes 27648 | tf_op jit(solution)/shard_map/all_gather | solution.py:24
  311.0 4.4 %all_gather.17 = bf16[4,4,1152]{2,1,0:T(4,128)(2,1)S(1)} all-gather(bf16[2,4,1152]{2,1,0:T(4,128)(2,1)S(1)} %all_gather.16), channel_id=1, replica_groups=mesh['crop'=2,'row_0'=2,'row_1'=4,'col_0'=8,'col_1'=2] {'col_1'}, dimensions={0}, use_global_device_ids=true | all-gather | bytes 55296 | tf_op jit(solution)/shard_map/all_gather | solution.py:24
  315.4 12.8 %all_gather.18 = bf16[16,4,1152]{2,1,0:T(4,128)(2,1)} all-gather(bf16[4,4,1152]{2,1,0:T(4,128)(2,1)S(1)} %all_gather.17), channel_id=1, replica_groups=mesh['crop'=2,'row_0'=2,'row_1'=4,'col_0'=8,'col_1'=2] {'row_1'}, dimensions={0}, use_global_device_ids=true | all-gather | bytes 184320 | tf_op jit(solution)/shard_map/all_gather | solution.py:24
  328.2 0.0 all-gather.5.cloned.1.call-update
  328.3 7.1 %all-to-all-start = ((bf16[16,3,24,128]{3,2,1,0:T(8,128)(2,1)}), bf16[16,3,24,128]{3,2,1,0:T(8,128)(2,1)S(1)}, u32[]{:S(2)}, u32[]{:S(2)}) async-start(bf16[16,3,24,128]{3,2,1,0:T(8,128)(2,1)} %bitcast.5), calls=%async_computation.1 | async-start | bytes 589824 | tf_op jit(solution)/shard_map/all_to_all | solution.py:158
  335.4 0.1 copy.94
  335.5 0.2 broadcast_in_dim.10
  335.7 0.3 reshape.139
  336.1 0.1 broadcast_and_fusion
  336.2 10.3 %all-to-all-done = bf16[16,3,24,128]{3,2,1,0:T(8,128)(2,1)S(1)} async-done(((bf16[16,3,24,128]{3,2,1,0:T(8,128)(2,1)}), bf16[16,3,24,128]{3,2,1,0:T(8,128)(2,1)S(1)}, u32[]{:S(2)}, u32[]{:S(2)}) %all-to-all-start) | async-done | bytes 294944 | tf_op jit(solution)/shard_map/all_to_all | solution.py:158
  346.6 0.4 convolution_convert_fusion
  347.0 0.9 fusion.51
  348.0 19.6 %all-gather.5.cloned.1.call-done = bf16[128,4,1152]{2,1,0:T(4,128)(2,1)} async-done(((bf16[16,4,1152]{2,1,0:T(4,128)(2,1)}), bf16[128,4,1152]{2,1,0:T(4,128)(2,1)}) %all-gather.5.cloned.1.call-update) | async-done | bytes 1179664 | tf_op jit(solution)/shard_map/all_gather | solution.py:24
  367.6 1.7 copy.96
  369.3 0.2 copy.97
  369.5 9.5 %reshape.148 = f32[4,8,16,48,24]{4,3,2,1,0:T(8,128)} reshape(f32[4,128,1152]{2,1,0:T(8,128)S(1)} %copy.97) | data formatting | bytes 4718592 | tf_op jit(solution)/shard_map/convert_element_type | solution.py:76
  379.0 10.7 %copy.98 = f32[4,8,48,16,24]{2,1,4,3,0:T(8,128)} copy(f32[4,8,48,16,24]{4,2,3,1,0:T(8,128)} %bitcast.76) | data formatting | bytes 4718592 | tf_op jit(solution)/shard_map/convert_element_type | solution.py:76
  389.7 4.8 %reshape.147 = f32[4,384,384]{1,2,0:T(8,128)S(1)} reshape(f32[4,8,48,16,24]{2,1,4,3,0:T(8,128)} %copy.98) | data formatting | bytes 4718592 | tf_op jit(solution)/shard_map/convert_element_type | solution.py:76
  394.4 6.6 %fusion.53 = (f32[3,4,384]{2,1,0:T(4,128)S(1)}, f32[3,4,384,384]{2,3,1,0:T(8,128)}) fusion(f32[4,384,384]{1,2,0:T(8,128)S(1)} %reshape.147, pred[384,384]{0,1:T(8,128)(4,1)S(1)} %broadcast_and_fusion, bf16[3,384,4,32]{1,3,2,0:T(8,128)(2,1)} %bitcast.87, bf16[3,384,4,32]{1,3,2,0:T(8,128)(2,1)} %bitcast.86), kind=kOutput, calls=%fused_computation.82 | convolution fusion | flops 122093952 | bytes 10192896 | tf_op jit(solution)/shard_map/sub | solution.py:79
  401.1 0.0 copy-start.1
  401.1 3.8 fusion.6
  404.9 0.2 copy.100
  405.1 0.3 fusion.19
  405.4 0.3 copy.101
  405.7 17.1 %all_to_all.30 = bf16[1,3,384,128]{3,1,0,2:T(4,128)(2,1)S(1)} all-to-all(bf16[1,3,384,128]{3,1,0,2:T(4,128)(2,1)S(1)} %copy.101), channel_id=1, replica_groups=mesh['crop'=2,'row_0'=2,'row_1'=4,'col_0'=8,'col_1'=2] {'col_0','col_1'}, dimensions={2} | all-to-all | bytes 589824 | tf_op jit(solution)/shard_map/all_to_all | solution.py:164
  422.8 1.0 fusion.18
  (32 shorter events, 0.2 us)
Async XLA Ops:
  6.5 3.5 copy-start
  6.5 68.6 %all-gather.3.cloned.1.call-start = ((), (), s32[]{:S(2)}) async-start(), calls=%async_computation.3 | async-start | bytes 2654208 | tf_op jit(solution)/shard_map/all_gather | solution.py:125
  12.7 284.2 %reduce-scatter.2.cloned.1.call-start = ((), (), s32[]{:S(2)}) async-start(), calls=%async_computation.4 | async-start | bytes 10027008 | tf_op jit(solution)/shard_map/reduce_scatter | solution.py:129
  93.7 1.0 copy-start.2
  93.7 1.0 copy-start.9
  93.7 1.0 copy-start.12
  93.7 206.3 %copy-start.10 = (f32[128]{0:T(128)S(1)}, f32[128]{0:T(128)}, u32[]{:S(2)}) copy-start(f32[128]{0:T(128)} %param.19) | copy-start | bytes 1540
  93.7 207.7 %copy-start.4 = (bf16[128,128]{1,0:T(8,128)(2,1)S(1)}, bf16[128,128]{1,0:T(8,128)(2,1)}, u32[]{:S(2)}) copy-start(bf16[128,128]{1,0:T(8,128)(2,1)} %param.20) | copy-start | bytes 98308
  93.8 208.6 %copy-start.11 = (f32[128]{0:T(128)S(1)}, f32[128]{0:T(128)}, u32[]{:S(2)}) copy-start(f32[128]{0:T(128)} %param.21) | copy-start | bytes 1540
  93.8 209.7 %copy-start.8 = (bf16[128,4]{0,1:T(4,128)(2,1)S(1)}, bf16[128,4]{0,1:T(4,128)(2,1)}, u32[]{:S(2)}) copy-start(bf16[128,4]{0,1:T(4,128)(2,1)} %param.24) | copy-start | bytes 3076
  93.8 241.6 %copy-start.7 = (s32[4,4]{1,0:T(4,128)S(1)}, s32[4,4]{1,0:T(4,128)}, u32[]{:S(2)}) copy-start(s32[4,4]{1,0:T(4,128)} %param.15) | copy-start | bytes 196
  93.8 242.2 %copy-start.6 = (s32[384]{0:T(512)S(1)}, s32[384]{0:T(512)}, u32[]{:S(2)}) copy-start(s32[384]{0:T(512)} %param.14) | copy-start | bytes 4612
  93.8 252.7 %copy-start.3 = (bf16[128,384]{1,0:T(8,128)(2,1)S(1)}, bf16[128,384]{1,0:T(8,128)(2,1)}, u32[]{:S(2)}) copy-start(bf16[128,384]{1,0:T(8,128)(2,1)} %param.22) | copy-start | bytes 294916
  93.8 273.8 %all-gather.5.cloned.1.call-start = ((), (), s32[]{:S(2)}) async-start(), calls=%async_computation.5 | async-start | bytes 1327104 | tf_op jit(solution)/shard_map/all_gather | solution.py:24
  328.3 18.3 %all-to-all-start = ((bf16[16,3,24,128]{3,2,1,0:T(8,128)(2,1)}), bf16[16,3,24,128]{3,2,1,0:T(8,128)(2,1)S(1)}, u32[]{:S(2)}, u32[]{:S(2)}) async-start(bf16[16,3,24,128]{3,2,1,0:T(8,128)(2,1)} %bitcast.5), calls=%async_computation.1 | async-start | bytes 589824 | tf_op jit(solution)/shard_map/all_to_all | solution.py:158
  401.0 4.0 copy-start.13
  401.0 21.8 %copy-start.5 = (bf16[128,128]{1,0:T(8,128)(2,1)S(1)}, bf16[128,128]{1,0:T(8,128)(2,1)}, u32[]{:S(2)}) copy-start(bf16[128,128]{1,0:T(8,128)(2,1)} %param.25) | copy-start | bytes 98308
  401.1 22.8 %copy-start.1 = (bf16[128,512]{1,0:T(8,128)(2,1)S(1)}, bf16[128,512]{1,0:T(8,128)(2,1)}, u32[]{:S(2)}) copy-start(bf16[128,512]{1,0:T(8,128)(2,1)} %param.17) | copy-start | bytes 393220
Sparse Core Ops, SparseCore 0:
  12.8 62.2 all-gather.2
  93.9 202.9 reduce-scatter.1
  328.4 39.1 all-gather.4
where the time goes:
time: 431 us; the launch traced here: 430 us
  waiting for transfers between devices  294 us (68%)
  local copies, waits for them, and re-layouts  44.4 us (10%)
  blocking collectives  40.2 us (9%)
  matrix products  21.2 us (5%)
  between operations  13.5 us (3%)
  other arithmetic  10.3 us (2%)
  starting transfers between devices  7.23 us (2%)
    reduce_scatter x1, waiting for transfers between devices, shards(): lax.psum_scatter(jnp.transpose(summed_part, (1, 2, 0)), COL, scatter_dime...  202 us
    all_gather x1, waiting for transfers between devices, shards(): right_columns = lax.all_gather(right_factor, ROW, axis=0, tiled=True)  61.9 us
    convert_element_type x5, local copies, waits for them, and re-layouts, attend_dense(): scores = scores + head_bias.astype(jnp.float32)[None]  26.8 us
    all_gather x3, blocking collectives, gather_in_order(): pieces = lax.all_gather(pieces, axes[k], axis=0, tiled=True)  23.1 us
    all_gather x1, waiting for transfers between devices, gather_in_order(): pieces = lax.all_gather(pieces, axes[k], axis=0, tiled=True)  19.6 us
    all_to_all x1, blocking collectives, shards(): lax.all_to_all(attended_rows, COL, split_axis=2, concat_axis=0, tiled=True)  17.1 us
    all_to_all x1, waiting for transfers between devices, shards(): lax.all_to_all(grouped, COL, split_axis=0, concat_axis=2, tiled=True)  10.3 us
    transpose x1, local copies, waits for them, and re-layouts, shards(): jnp.transpose(summed_part, (1, 2, 0))  9.81 us
  transfers between devices with their start and end apart: 4, of which 4 were waited for; matrix products, arithmetic and copies ran while one was open for 1% of the time, Pallas kernels for 0%

commit v1 on v0

--- a/solution.py
+++ b/solution.py
@@ -122,7 +122,10 @@
         * jax.nn.sigmoid(projected[..., 2 * channels : 3 * channels])
         * projected[..., 3 * channels :]
     ).astype(jnp.bfloat16)
-    right_columns = lax.all_gather(right_factor, ROW, axis=0, tiled=True)
+    n_dev = lax.axis_size(ROW)
+    parts = jnp.stack([right_factor for _ in range(n_dev)])
+    parts = lax.all_to_all(parts, ROW, split_axis=0, concat_axis=0)
+    right_columns = jnp.concatenate(parts, axis=0)
     summed_part = lax.dot_general(
         right_columns, left_factor, (((1,), (1,)), ((2,), (2,))), preferred_element_type=jnp.float32
     )

time: 431 us -> 410 us (0.951)
  waiting for transfers between devices: 294 us -> 260 us
  starting transfers between devices: 7.23 us -> 14.6 us
    all_gather x1 -> x0, waiting for transfers between devices: 61.9 us -> none  [shards(): right_columns = lax.all_gather(right_factor, ROW, axis=0, tiled=True)]
    all_to_all x0 -> x1, waiting for transfers between devices: none -> 27.1 us  [shards(): parts = lax.all_to_all(parts, ROW, split_axis=0, concat_axis=0)]
    all_to_all x0 -> x1, starting transfers between devices: none -> 7.37 us  [shards(): parts = lax.all_to_all(parts, ROW, split_axis=0, concat_axis=0)]
where the time goes in v1:
time: 410 us; the launch traced here: 409 us
  waiting for transfers between devices  260 us (63%)
  local copies, waits for them, and re-layouts  46.8 us (11%)
  blocking collectives  40.2 us (10%)
  matrix products  22.9 us (6%)
  starting transfers between devices  14.6 us (4%)
  between operations  13.7 us (3%)
  other arithmetic  10.3 us (3%)
    reduce_scatter x1, waiting for transfers between devices, shards(): lax.psum_scatter(jnp.transpose(summed_part, (1, 2, 0)), COL, scatter_dime...  203 us
    all_to_all x1, waiting for transfers between devices, shards(): parts = lax.all_to_all(parts, ROW, split_axis=0, concat_axis=0)  27.1 us
    convert_element_type x5, local copies, waits for them, and re-layouts, attend_dense(): scores = scores + head_bias.astype(jnp.float32)[None]  26.8 us
    all_gather x3, blocking collectives, gather_in_order(): pieces = lax.all_gather(pieces, axes[k], axis=0, tiled=True)  23.1 us
    all_gather x1, waiting for transfers between devices, gather_in_order(): pieces = lax.all_gather(pieces, axes[k], axis=0, tiled=True)  19.6 us
    all_to_all x1, blocking collectives, shards(): lax.all_to_all(attended_rows, COL, split_axis=2, concat_axis=0, tiled=True)  17.1 us
    all_to_all x1, waiting for transfers between devices, shards(): lax.all_to_all(grouped, COL, split_axis=0, concat_axis=2, tiled=True)  10.3 us
    transpose x1, local copies, waits for them, and re-layouts, shards(): jnp.transpose(summed_part, (1, 2, 0))  9.78 us
  transfers between devices with their start and end apart: 4, of which 4 were waited for; matrix products, arithmetic and copies ran while one was open for 1% of the time, Pallas kernels for 0%

profile of v1, /device:TPU:8, one launch (start us, length us, event | category | flops | bytes accessed | tf_op | source)
XLA Modules:
  0.0 408.9 jit_solution(8401492152655466099)
XLA Ops:
  6.5 0.7 convert_element_type.68
  7.3 0.1 dynamic_slice.6
  7.3 0.1 dynamic_slice.7
  7.4 1.2 convert_reduce_fusion
  8.6 1.4 fusion.25
  10.0 0.1 broadcast_multiply_fusion
  10.1 1.5 fusion.39
  11.6 1.1 fusion.28
  12.7 1.7 stack.2
  14.4 7.4 %all-to-all-start = ((bf16[8,48,24,128]{3,2,1,0:T(8,128)(2,1)}), bf16[8,48,24,128]{3,2,1,0:T(8,128)(2,1)S(1)}, u32[]{:S(2)}, u32[]{:S(2)}) async-start(bf16[8,48,24,128]{3,2,1,0:T(8,128)(2,1)} %stack.2), calls=%async_computation | async-start | bytes 4718592 | tf_op jit(solution)/shard_map/all_to_all | solution.py:127
  21.8 1.5 copy.85
  23.3 27.1 %all-to-all-done = bf16[8,48,24,128]{3,2,1,0:T(8,128)(2,1)S(1)} async-done(((bf16[8,48,24,128]{3,2,1,0:T(8,128)(2,1)}), bf16[8,48,24,128]{3,2,1,0:T(8,128)(2,1)S(1)}, u32[]{:S(2)}, u32[]{:S(2)}) %all-to-all-start) | async-done | bytes 2359328 | tf_op jit(solution)/shard_map/all_to_all | solution.py:127
  50.4 3.4 copy.84
  53.8 6.7 %convolution_bitcast_fusion = f32[384,48,128]{0,1,2:T(8,128)} fusion(bf16[384,24,128]{0,1,2:T(8,128)(2,1)} %copy.84, bf16[48,24,128]{0,1,2:T(8,128)(2,1)S(1)} %copy.85), kind=kOutput, calls=%fused_computation.10 | convolution fusion | flops 113246208 | bytes 12091392 | tf_op jit(solution)/shard_map/dot_general | solution.py:129
  60.5 9.8 %copy.86 = f32[384,48,128]{2,1,0:T(8,128)} copy(f32[384,48,128]{0,1,2:T(8,128)} %convolution_bitcast_fusion) | data formatting | bytes 18874368 | tf_op jit(solution)/shard_map/transpose | solution.py:133
  70.3 0.0 copy-start.4
  70.3 0.0 copy-start.11
  70.3 0.0 copy-start.8
  70.3 0.0 reduce-scatter.2.cloned.1.call-update
  70.4 0.0 copy-start.7
  70.4 0.0 copy-start.6
  70.4 0.0 copy-start.3
  70.4 0.0 all-gather.2.cloned.1.call-start
  70.4 0.8 copy-done.2
  71.2 0.5 fusion.14
  71.8 203.3 %reduce-scatter.2.cloned.1.call-done = f32[24,48,128]{2,1,0:T(8,128)} async-done(((f32[384,48,128]{2,1,0:T(8,128)}), f32[24,48,128]{2,1,0:T(8,128)}) %reduce-scatter.2.cloned.1.call-update) | async-done | bytes 589840 | tf_op jit(solution)/shard_map/reduce_scatter | solution.py:132
  275.1 1.3 bitcast_reduce_fusion
  276.4 0.1 copy.87
  276.5 0.1 copy.88
  276.6 1.5 multiply_reduce_fusion.1
  278.1 0.1 copy.89
  278.2 0.1 copy.90
  278.2 1.4 multiply_convert_fusion.1
  279.7 0.4 fusion.52
  280.1 0.4 multiply_reduce_fusion
  280.5 1.1 multiply_convert_fusion
  281.6 1.6 fusion.20
  283.2 0.1 broadcast_in_dim_reshape.3
  283.3 5.9 %all_gather.12 = bf16[2,4,1152]{2,1,0:T(4,128)(2,1)S(1)} all-gather(bf16[1,4,1152]{2,1,0:T(4,128)(2,1)S(1)} %broadcast_in_dim_reshape.3), channel_id=1, replica_groups=mesh['crop'=2,'row_0'=2,'row_1'=4,'col_0'=8,'col_1'=2] {'row_0'}, dimensions={0}, use_global_device_ids=true | all-gather | bytes 27648 | tf_op jit(solution)/shard_map/all_gather | solution.py:24
  289.2 4.4 %all_gather.13 = bf16[4,4,1152]{2,1,0:T(4,128)(2,1)S(1)} all-gather(bf16[2,4,1152]{2,1,0:T(4,128)(2,1)S(1)} %all_gather.12), channel_id=1, replica_groups=mesh['crop'=2,'row_0'=2,'row_1'=4,'col_0'=8,'col_1'=2] {'col_1'}, dimensions={0}, use_global_device_ids=true | all-gather | bytes 55296 | tf_op jit(solution)/shard_map/all_gather | solution.py:24
  293.6 12.8 %all_gather.14 = bf16[16,4,1152]{2,1,0:T(4,128)(2,1)} all-gather(bf16[4,4,1152]{2,1,0:T(4,128)(2,1)S(1)} %all_gather.13), channel_id=1, replica_groups=mesh['crop'=2,'row_0'=2,'row_1'=4,'col_0'=8,'col_1'=2] {'row_1'}, dimensions={0}, use_global_device_ids=true | all-gather | bytes 184320 | tf_op jit(solution)/shard_map/all_gather | solution.py:24
  306.4 0.0 all-gather.2.cloned.1.call-update
  306.5 7.1 %all-to-all-start.1 = ((bf16[16,3,24,128]{3,2,1,0:T(8,128)(2,1)}), bf16[16,3,24,128]{3,2,1,0:T(8,128)(2,1)S(1)}, u32[]{:S(2)}, u32[]{:S(2)}) async-start(bf16[16,3,24,128]{3,2,1,0:T(8,128)(2,1)} %bitcast.6), calls=%async_computation.2 | async-start | bytes 589824 | tf_op jit(solution)/shard_map/all_to_all | solution.py:161
  313.6 0.1 copy.94
  313.7 0.2 broadcast_in_dim.10
  313.9 0.3 reshape.145
  314.3 0.1 broadcast_and_fusion
  314.4 10.3 %all-to-all-done.1 = bf16[16,3,24,128]{3,2,1,0:T(8,128)(2,1)S(1)} async-done(((bf16[16,3,24,128]{3,2,1,0:T(8,128)(2,1)}), bf16[16,3,24,128]{3,2,1,0:T(8,128)(2,1)S(1)}, u32[]{:S(2)}, u32[]{:S(2)}) %all-to-all-start.1) | async-done | bytes 294944 | tf_op jit(solution)/shard_map/all_to_all | solution.py:161
  324.8 0.4 convolution_convert_fusion
  325.2 0.9 fusion.51
  326.2 19.6 %all-gather.2.cloned.1.call-done = bf16[128,4,1152]{2,1,0:T(4,128)(2,1)} async-done(((bf16[16,4,1152]{2,1,0:T(4,128)(2,1)}), bf16[128,4,1152]{2,1,0:T(4,128)(2,1)}) %all-gather.2.cloned.1.call-update) | async-done | bytes 1179664 | tf_op jit(solution)/shard_map/all_gather | solution.py:24
  345.8 1.7 copy.96
  347.6 0.2 copy.97
  347.7 9.5 %reshape.154 = f32[4,8,16,48,24]{4,3,2,1,0:T(8,128)} reshape(f32[4,128,1152]{2,1,0:T(8,128)S(1)} %copy.97) | data formatting | bytes 4718592 | tf_op jit(solution)/shard_map/convert_element_type | solution.py:76
  357.2 10.7 %copy.98 = f32[4,8,48,16,24]{2,1,4,3,0:T(8,128)} copy(f32[4,8,48,16,24]{4,2,3,1,0:T(8,128)} %bitcast.77) | data formatting | bytes 4718592 | tf_op jit(solution)/shard_map/convert_element_type | solution.py:76
  367.9 4.8 %reshape.153 = f32[4,384,384]{1,2,0:T(8,128)S(1)} reshape(f32[4,8,48,16,24]{2,1,4,3,0:T(8,128)} %copy.98) | data formatting | bytes 4718592 | tf_op jit(solution)/shard_map/convert_element_type | solution.py:76
  372.7 6.6 %fusion.53 = (f32[3,4,384]{2,1,0:T(4,128)S(1)}, f32[3,4,384,384]{2,3,1,0:T(8,128)}) fusion(f32[4,384,384]{1,2,0:T(8,128)S(1)} %reshape.153, pred[384,384]{0,1:T(8,128)(4,1)S(1)} %broadcast_and_fusion, bf16[3,384,4,32]{1,3,2,0:T(8,128)(2,1)} %bitcast.89, bf16[3,384,4,32]{1,3,2,0:T(8,128)(2,1)} %bitcast.88), kind=kOutput, calls=%fused_computation.82 | convolution fusion | flops 122093952 | bytes 10192896 | tf_op jit(solution)/shard_map/sub | solution.py:79
  379.3 0.0 copy-start.1
  379.3 3.8 fusion.6
  383.1 0.2 copy.100
  383.3 0.3 fusion.19
  383.6 0.3 copy.101
  383.9 17.1 %all_to_all.35 = bf16[1,3,384,128]{3,1,0,2:T(4,128)(2,1)S(1)} all-to-all(bf16[1,3,384,128]{3,1,0,2:T(4,128)(2,1)S(1)} %copy.101), channel_id=1, replica_groups=mesh['crop'=2,'row_0'=2,'row_1'=4,'col_0'=8,'col_1'=2] {'col_0','col_1'}, dimensions={2} | all-to-all | bytes 589824 | tf_op jit(solution)/shard_map/all_to_all | solution.py:167
  401.0 1.0 fusion.18
  (32 shorter events, 0.2 us)
Async XLA Ops:
  6.5 3.5 copy-start
  14.4 36.0 %all-to-all-start = ((bf16[8,48,24,128]{3,2,1,0:T(8,128)(2,1)}), bf16[8,48,24,128]{3,2,1,0:T(8,128)(2,1)S(1)}, u32[]{:S(2)}, u32[]{:S(2)}) async-start(bf16[8,48,24,128]{3,2,1,0:T(8,128)(2,1)} %stack.2), calls=%async_computation | async-start | bytes 4718592 | tf_op jit(solution)/shard_map/all_to_all | solution.py:127
  21.8 253.4 %reduce-scatter.2.cloned.1.call-start = ((), (), s32[]{:S(2)}) async-start(), calls=%async_computation.4 | async-start | bytes 10027008 | tf_op jit(solution)/shard_map/reduce_scatter | solution.py:132
  70.3 1.0 copy-start.2
  70.3 1.0 copy-start.9
  70.3 1.0 copy-start.12
  70.3 207.9 %copy-start.10 = (f32[128]{0:T(128)S(1)}, f32[128]{0:T(128)}, u32[]{:S(2)}) copy-start(f32[128]{0:T(128)} %param.19) | copy-start | bytes 1540
  70.3 209.4 %copy-start.4 = (bf16[128,128]{1,0:T(8,128)(2,1)S(1)}, bf16[128,128]{1,0:T(8,128)(2,1)}, u32[]{:S(2)}) copy-start(bf16[128,128]{1,0:T(8,128)(2,1)} %param.20) | copy-start | bytes 98308
  70.3 210.2 %copy-start.11 = (f32[128]{0:T(128)S(1)}, f32[128]{0:T(128)}, u32[]{:S(2)}) copy-start(f32[128]{0:T(128)} %param.21) | copy-start | bytes 1540
  70.3 211.3 %copy-start.8 = (bf16[128,4]{0,1:T(4,128)(2,1)S(1)}, bf16[128,4]{0,1:T(4,128)(2,1)}, u32[]{:S(2)}) copy-start(bf16[128,4]{0,1:T(4,128)(2,1)} %param.24) | copy-start | bytes 3076
  70.4 243.3 %copy-start.7 = (s32[4,4]{1,0:T(4,128)S(1)}, s32[4,4]{1,0:T(4,128)}, u32[]{:S(2)}) copy-start(s32[4,4]{1,0:T(4,128)} %param.15) | copy-start | bytes 196
  70.4 243.9 %copy-start.6 = (s32[384]{0:T(512)S(1)}, s32[384]{0:T(512)}, u32[]{:S(2)}) copy-start(s32[384]{0:T(512)} %param.14) | copy-start | bytes 4612
  70.4 254.4 %copy-start.3 = (bf16[128,384]{1,0:T(8,128)(2,1)S(1)}, bf16[128,384]{1,0:T(8,128)(2,1)}, u32[]{:S(2)}) copy-start(bf16[128,384]{1,0:T(8,128)(2,1)} %param.22) | copy-start | bytes 294916
  70.4 275.4 %all-gather.2.cloned.1.call-start = ((), (), s32[]{:S(2)}) async-start(), calls=%async_computation.5 | async-start | bytes 1327104 | tf_op jit(solution)/shard_map/all_gather | solution.py:24
  306.5 18.3 %all-to-all-start.1 = ((bf16[16,3,24,128]{3,2,1,0:T(8,128)(2,1)}), bf16[16,3,24,128]{3,2,1,0:T(8,128)(2,1)S(1)}, u32[]{:S(2)}, u32[]{:S(2)}) async-start(bf16[16,3,24,128]{3,2,1,0:T(8,128)(2,1)} %bitcast.6), calls=%async_computation.2 | async-start | bytes 589824 | tf_op jit(solution)/shard_map/all_to_all | solution.py:161
  379.3 4.0 copy-start.13
  379.3 21.8 %copy-start.5 = (bf16[128,128]{1,0:T(8,128)(2,1)S(1)}, bf16[128,128]{1,0:T(8,128)(2,1)}, u32[]{:S(2)}) copy-start(bf16[128,128]{1,0:T(8,128)(2,1)} %param.25) | copy-start | bytes 98308
  379.3 22.8 %copy-start.1 = (bf16[128,512]{1,0:T(8,128)(2,1)S(1)}, bf16[128,512]{1,0:T(8,128)(2,1)}, u32[]{:S(2)}) copy-start(bf16[128,512]{1,0:T(8,128)(2,1)} %param.17) | copy-start | bytes 393220
Sparse Core Ops, SparseCore 0:
  70.5 204.6 reduce-scatter.1
  306.6 39.1 all-gather.1
